TPU v7x, 256 devices: a whole 4x4x8 slice. The times are simulated.
256 devices in a mesh: row: 8 (over z), col: 32 (over y, x, core).
Axes of the slice: x: 4, y: 4, z: 8, core: 2. Of those that a mesh axis runs over, the one named last changes fastest.
Arguments:
- amps: bfloat16 [384, 131072], P('row', 'col'), may hold values from -6 to 6
- integrals: bfloat16 [131072, 8192], P('col', 'row'), may hold values from -0.046875 to 0.046875
- cd_first: int32 [131072], P('col'), may hold values from 0 to 2399
- cd_second: int32 [131072], P('col'), may hold values from 0 to 2399
- ab_first: int32 [8192], P('row'), may hold values from 0 to 2399
- ab_second: int32 [8192], P('row'), may hold values from 0 to 2399
- occ_first: int32 [384], P('col'), may hold values from 0 to 199
- occ_second: int32 [384], P('col'), may hold values from 0 to 199
- virt_irrep: int32 [2400], replicated, may hold values from 0 to 7
- occ_energy: float32 [200], replicated, may hold values from -2 to -0.5
- virt_energy: float32 [2400], replicated, may hold values from 0.2 to 3
Outputs:
- update: float32 [384, 8192], P('col', 'row')
All inputs are finite; a program needn't handle non-finite values.
Results may differ from a plain program's by a relative error of at most 0.0003.
Values may be sent and summed in bfloat16 or wider, within the bound.
No kernel may reach another device: no remote copies, remote signals or barrier semaphores. Data moves between devices by JAX's collectives and lax.ppermute only.
A program may use at most 64 MiB of HBM per device.

v0:
```python
import jax
import jax.numpy as jnp
from jax import lax
from jax.sharding import PartitionSpec as P


def table_lookup(values_table, positions):
    row_width = 64
    row_count = -(-values_table.shape[0] // row_width)
    padded_table = jnp.pad(
        values_table, (0, row_count * row_width - values_table.shape[0])
    ).reshape(row_count, row_width)
    high_hot = (
        (positions // row_width)[:, None] == jnp.arange(row_count, dtype=jnp.int32)[None, :]
    ).astype(jnp.float32)
    low_hot = (
        (positions % row_width)[:, None] == jnp.arange(row_width, dtype=jnp.int32)[None, :]
    ).astype(jnp.float32)
    picked = jnp.dot(
        high_hot, padded_table, precision=lax.Precision.HIGHEST, preferred_element_type=jnp.float32
    )
    return jnp.sum(picked * low_hot, axis=1)


def irrep_of(labels_float, first_orb, second_orb):
    first_label = table_lookup(labels_float, first_orb).astype(jnp.int32)
    second_label = table_lookup(labels_float, second_orb).astype(jnp.int32)
    return jnp.bitwise_xor(first_label, second_label)


def on_device(
    amps,
    integrals,
    cd_first,
    cd_second,
    ab_first,
    ab_second,
    occ_first,
    occ_second,
    virt_irrep,
    occ_energy,
    virt_energy,
):
    labels_float = virt_irrep.astype(jnp.float32)
    irrep_cd = irrep_of(labels_float, cd_first, cd_second)
    irrep_ab = irrep_of(labels_float, ab_first, ab_second)
    masked = jnp.where(irrep_cd[:, None] == irrep_ab[None, :], integrals, jnp.zeros_like(integrals))
    partial_sums = jnp.dot(
        lax.all_gather(amps, "row", axis=0, tiled=True), masked, preferred_element_type=jnp.float32
    )
    own_rows = occ_first.shape[0]
    summed = lax.psum(partial_sums, "col")
    ladder = lax.dynamic_slice_in_dim(summed, lax.axis_index("col") * own_rows, own_rows, 0)
    virt_part = table_lookup(virt_energy, ab_first) + table_lookup(virt_energy, ab_second)
    occ_part = table_lookup(occ_energy, occ_first) + table_lookup(occ_energy, occ_second)
    denom = virt_part[None, :] - occ_part[:, None]
    return ladder / denom


def solution(mesh):
    in_specs = (
        P("row", "col"),
        P("col", "row"),
        P("col"),
        P("col"),
        P("row"),
        P("row"),
        P("col"),
        P("col"),
        P(),
        P(),
        P(),
    )
    out_specs = P("col", "row")
    return jax.shard_map(
        on_device, mesh=mesh, in_specs=in_specs, out_specs=out_specs, check_vma=False
    )
```

profile of v0, /device:TPU:6, one launch (start us, length us, event | category | flops | bytes accessed | tf_op | source)
XLA Modules:
  0.0 190.4 jit_solution(7204045527473177920)
XLA Ops:
  6.5 0.0 all-gather.2.cloned.1.call-start
  6.5 0.7 all-gather.2.cloned.1.call-update
  7.3 0.0 all-reduce.5.cloned.1.call-start
  7.3 0.7 convert_element_type.57
  8.0 0.1 reshape.50
  8.1 0.7 add_select_fusion.5
  8.8 0.6 fusion.8
  9.4 0.7 add_select_fusion.7
  10.1 0.6 fusion.7
  10.7 0.7 add_select_fusion.2
  11.4 0.7 fusion.5
  12.1 0.7 add_select_fusion
  12.8 0.7 fusion.6
  13.5 0.0 copy-start.2
  13.6 0.0 copy-start.1
  13.6 0.0 copy-start
  13.6 0.0 copy-start.3
  13.6 43.5 %all-gather.2.cloned.1.call-done = bf16[384,4096]{1,0:T(8,128)(2,1)} async-done(((bf16[48,4096]{1,0:T(8,128)(2,1)}), bf16[384,4096]{1,0:T(8,128)(2,1)}) %all-gather.2.cloned.1.call-update) | async-done | bytes 3145744 | tf_op jit(solution)/shard_map/all_gather | solution.py:49
  57.1 9.0 %fusion.4 = f32[384,1024]{1,0:T(8,128)} fusion(bf16[384,4096]{1,0:T(8,128)(2,1)} %all-gather.2.cloned.1.call-done, bf16[4096,1024]{1,0:T(8,128)(2,1)} %param.12, s32[1024]{0:T(1024)S(1)} %convert_xor_fusion.1, s32[4096]{0:T(1024)S(1)} %convert_xor_fusion), kind=kOutput, calls=%fused_computation.7 | convolution fusion | flops 3229614080 | bytes 13127680 | tf_op jit(solution)/shard_map/dot_general | solution.py:48
  66.1 0.0 all-reduce.5.cloned.1.call-update
  66.1 0.0 copy-done.2
  66.1 0.0 copy-done.1
  66.2 0.1 reshape.52
  66.2 0.0 copy-done
  66.2 0.1 reshape.51
  66.3 0.3 fusion.11
  66.6 0.0 copy-done.3
  66.6 0.3 fusion.12
  67.0 0.6 fusion.10
  67.5 0.6 fusion.9
  68.1 113.8 %all-reduce.5.cloned.1.call-done = f32[384,1024]{1,0:T(8,128)} async-done(((f32[384,1024]{1,0:T(8,128)}), f32[384,1024]{1,0:T(8,128)}) %all-reduce.5.cloned.1.call-update) | async-done | bytes 1572880 | tf_op jit(solution)/shard_map/psum | solution.py:52
  181.9 1.6 subtract_divide_fusion
  (9 shorter events, 0.1 us)
Async XLA Ops:
  6.5 50.5 %all-gather.2.cloned.1.call-start = ((), (), s32[]{:S(2)}) async-start(), calls=%async_computation | async-start | bytes 3538944 | tf_op jit(solution)/shard_map/all_gather | solution.py:49
  7.3 174.7 %all-reduce.5.cloned.1.call-start = ((), (), s32[]{:S(2)}) async-start(), calls=%async_computation.1 | async-start | bytes 3145728 | tf_op jit(solution)/shard_map/psum | solution.py:52
  13.5 52.5 %copy-start.2 = (s32[12]{0:T(128)S(1)}, s32[12]{0:T(128)}, u32[]{:S(2)}) copy-start(s32[12]{0:T(128)} %param.17) | copy-start | bytes 148
  13.6 52.6 %copy-start.1 = (f32[200]{0:T(256)S(1)}, f32[200]{0:T(256)}, u32[]{:S(2)}) copy-start(f32[200]{0:T(256)} %param.20) | copy-start | bytes 2404
  13.6 52.7 %copy-start = (f32[2400]{0:T(1024)S(1)}, f32[2400]{0:T(1024)}, u32[]{:S(2)}) copy-start(f32[2400]{0:T(1024)} %param.21) | copy-start | bytes 28804
  13.6 53.0 %copy-start.3 = (s32[12]{0:T(128)S(1)}, s32[12]{0:T(128)}, u32[]{:S(2)}) copy-start(s32[12]{0:T(128)} %param.18) | copy-start | bytes 148
Sparse Core Ops, SparseCore 0:
  9.1 47.8 all-gather.1
  66.2 115.6 all-reduce.4
where the time goes:
time: 191 us; the launch traced here: 190 us
  waiting for transfers between devices  158 us (83%)
  between operations  13.5 us (7%)
  matrix products  13.3 us (7%)
  other arithmetic  5.24 us (3%)
    psum x1, waiting for transfers between devices, on_device(): summed = lax.psum(partial_sums, 'col')  114 us
    all_gather x1, waiting for transfers between devices, on_device(): lax.all_gather(amps, 'row', axis=0, tiled=True)  43.5 us
    dot_general x1, matrix products, on_device(): jnp.dot(lax.all_gather(amps, 'row', axis=0, tiled=True), masked, preferre...  9 us
    dot_general x8, matrix products, table_lookup(): jnp.dot(high_hot, padded_table, precision=lax.Precision.HIGHEST, preferre...  4.28 us
  transfers between devices with their start and end apart: 2, of which 2 were waited for; matrix products, arithmetic and copies ran while one was open for 4% of the time, Pallas kernels for 0%

commit v1 on v0

--- a/solution.py
+++ b/solution.py
@@ -41,13 +41,17 @@
     occ_energy,
     virt_energy,
 ):
+
+    def _post_spans(page):
+        return jnp.concatenate(
+            lax.all_to_all(jnp.stack([page] * lax.axis_size("row"), 0), "row", 0, 0), 0
+        )
+
     labels_float = virt_irrep.astype(jnp.float32)
     irrep_cd = irrep_of(labels_float, cd_first, cd_second)
     irrep_ab = irrep_of(labels_float, ab_first, ab_second)
     masked = jnp.where(irrep_cd[:, None] == irrep_ab[None, :], integrals, jnp.zeros_like(integrals))
-    partial_sums = jnp.dot(
-        lax.all_gather(amps, "row", axis=0, tiled=True), masked, preferred_element_type=jnp.float32
-    )
+    partial_sums = jnp.dot(_post_spans(amps), masked, preferred_element_type=jnp.float32)
     own_rows = occ_first.shape[0]
     summed = lax.psum(partial_sums, "col")
     ladder = lax.dynamic_slice_in_dim(summed, lax.axis_index("col") * own_rows, own_rows, 0)

time: 191 us -> 222 us (1.16)
  waiting for transfers between devices: 158 us -> 182 us
  starting transfers between devices: 0.04 us -> 8.63 us
  other arithmetic: 5.24 us -> 1.72 us
  local copies, waits for them, and re-layouts: 0.27 us -> 3.33 us
    all_to_all x0 -> x1, waiting for transfers between devices: none -> 71 us  [_post_spans(): lax.all_to_all(jnp.stack([page] * lax.axis_size('row'), 0), 'row', 0, 0)]
    all_gather x1 -> x0, waiting for transfers between devices: 43.5 us -> none  [on_device(): lax.all_gather(amps, 'row', axis=0, tiled=True)]
    all_to_all x0 -> x1, starting transfers between devices: none -> 8.6 us  [_post_spans(): lax.all_to_all(jnp.stack([page] * lax.axis_size('row'), 0), 'row', 0, 0)]
    another operation x0 -> x1, local copies, waits for them, and re-layouts: none -> 3.06 us  [_post_spans(): jnp.stack([page] * lax.axis_size('row'), 0)]
    psum x1, waiting for transfers between devices: 114 us -> 111 us  [on_device(): summed = lax.psum(partial_sums, 'col')]
  transfers between devices with their start and end apart: 2 -> 2, of which waited for: 2 -> 2; matrix products, arithmetic and copies ran while one was open for 4% -> 2% of each run, Pallas kernels for 0% -> 0%
where the time goes in v1:
time: 222 us
  waiting for transfers between devices  182 us (82%)
  between operations  13.6 us (6%)
  matrix products  12.4 us (6%)
  starting transfers between devices  8.63 us (4%)
  local copies, waits for them, and re-layouts  3.33 us (2%)
    psum x1, waiting for transfers between devices, on_device(): summed = lax.psum(partial_sums, 'col')  111 us
    all_to_all x1, waiting for transfers between devices, _post_spans(): lax.all_to_all(jnp.stack([page] * lax.axis_size('row'), 0), 'row', 0, 0)  71 us
    all_to_all x1, starting transfers between devices, _post_spans(): lax.all_to_all(jnp.stack([page] * lax.axis_size('row'), 0), 'row', 0, 0)  8.6 us
    dot_general x1, matrix products, on_device(): jnp.dot(_post_spans(amps), masked, preferred_element_type=jnp.float32)  8.1 us
  transfers between devices with their start and end apart: 2, of which 2 were waited for; matrix products, arithmetic and copies ran while one was open for 2% of the time, Pallas kernels for 0%

profile of v1, /device:TPU:6, one launch (start us, length us, event | category | flops | bytes accessed | tf_op | source)
XLA Modules:
  0.0 222.1 jit_solution(7581456613052457535)
XLA Ops:
  6.5 0.0 copy-start.2
  6.5 0.0 copy-start.4
  6.5 3.1 %stack.2 = bf16[8,48,4096]{2,1,0:T(8,128)(2,1)} broadcast(bf16[48,4096]{1,0:T(8,128)(2,1)} %param.11), dimensions={1,2} | broadcast | bytes 3538944 | tf_op jit(solution)/shard_map/stack | solution.py:47
  9.6 0.0 copy-start.5
  9.6 0.0 copy-start
  9.6 8.6 %all-to-all-start = ((bf16[8,48,4096]{2,1,0:T(8,128)(2,1)}), bf16[8,48,4096]{2,1,0:T(8,128)(2,1)S(1)}, u32[]{:S(2)}, u32[]{:S(2)}) async-start(bf16[8,48,4096]{2,1,0:T(8,128)(2,1)} %stack.2), calls=%async_computation | async-start | bytes 6291456 | tf_op jit(solution)/shard_map/all_to_all | solution.py:47
  18.2 0.0 all-reduce.5.cloned.1.call-start
  18.2 0.0 copy-done.2
  18.3 0.1 reshape.55
  18.4 0.0 copy-done.4
  18.4 0.6 fusion.8
  18.9 0.0 copy-done.5
  19.0 0.6 fusion.7
  19.6 0.0 copy-done
  19.6 0.7 fusion.6
  20.3 0.0 copy-done.1
  20.3 0.7 fusion.5
  21.0 71.0 %all-to-all-done = bf16[8,48,4096]{2,1,0:T(8,128)(2,1)S(1)} async-done(((bf16[8,48,4096]{2,1,0:T(8,128)(2,1)}), bf16[8,48,4096]{2,1,0:T(8,128)(2,1)S(1)}, u32[]{:S(2)}, u32[]{:S(2)}) %all-to-all-start) | async-done | bytes 3145760 | tf_op jit(solution)/shard_map/all_to_all | solution.py:47
  92.0 8.1 %fusion.4 = f32[384,1024]{1,0:T(8,128)} fusion(bf16[384,4096]{1,0:T(8,128)(2,1)S(1)} %bitcast.12, bf16[4096,1024]{1,0:T(8,128)(2,1)} %param.12, s32[1024]{0:T(1024)S(1)} %convert_xor_fusion.1, s32[4096]{0:T(1024)S(1)} %convert_xor_fusion), kind=kOutput, calls=%fused_computation.7 | convolution fusion | flops 3229614080 | bytes 13127680 | tf_op jit(solution)/shard_map/dot_general | solution.py:54
  100.1 0.0 all-reduce.5.cloned.1.call-update
  100.1 0.0 copy-done.7
  100.2 0.0 copy-done.6
  100.2 0.1 reshape.58
  100.3 0.0 copy-done.3
  100.3 0.1 reshape.57
  100.3 0.3 fusion.11
  100.6 0.0 copy-done.8
  100.7 0.3 fusion.12
  101.0 0.6 fusion.9
  101.6 0.6 fusion.10
  102.2 111.5 %all-reduce.5.cloned.1.call-done = f32[384,1024]{1,0:T(8,128)} async-done(((f32[384,1024]{1,0:T(8,128)}), f32[384,1024]{1,0:T(8,128)}) %all-reduce.5.cloned.1.call-update) | async-done | bytes 1572880 | tf_op jit(solution)/shard_map/psum | solution.py:56
  213.6 1.6 subtract_divide_fusion
  (19 shorter events, 0.1 us)
Async XLA Ops:
  6.5 11.7 %copy-start.2 = (s32[2400]{0:T(1024)S(1)}, s32[2400]{0:T(1024)}, u32[]{:S(2)}) copy-start(s32[2400]{0:T(1024)} %param.19) | copy-start | bytes 28804
  6.5 11.8 %copy-start.4 = (s32[1024]{0:T(1024)S(1)}, s32[1024]{0:T(1024)}, u32[]{:S(2)}) copy-start(s32[1024]{0:T(1024)} %param.16) | copy-start | bytes 12292
  9.6 9.4 %copy-start.5 = (s32[1024]{0:T(1024)S(1)}, s32[1024]{0:T(1024)}, u32[]{:S(2)}) copy-start(s32[1024]{0:T(1024)} %param.15) | copy-start | bytes 12292
  9.6 10.0 %copy-start = (s32[4096]{0:T(1024)S(1)}, s32[4096]{0:T(1024)}, u32[]{:S(2)}) copy-start(s32[4096]{0:T(1024)} %param.14) | copy-start | bytes 49156
  9.6 10.7 %copy-start.1 = (s32[4096]{0:T(1024)S(1)}, s32[4096]{0:T(1024)}, u32[]{:S(2)}) copy-start(s32[4096]{0:T(1024)} %param.13) | copy-start | bytes 49156
  9.6 82.4 %all-to-all-start = ((bf16[8,48,4096]{2,1,0:T(8,128)(2,1)}), bf16[8,48,4096]{2,1,0:T(8,128)(2,1)S(1)}, u32[]{:S(2)}, u32[]{:S(2)}) async-start(bf16[8,48,4096]{2,1,0:T(8,128)(2,1)} %stack.2), calls=%async_computation | async-start | bytes 6291456 | tf_op jit(solution)/shard_map/all_to_all | solution.py:47
  18.2 195.4 %all-reduce.5.cloned.1.call-start = ((), (), s32[]{:S(2)}) async-start(), calls=%async_computation.1 | async-start | bytes 3145728 | tf_op jit(solution)/shard_map/psum | solution.py:56
  92.0 8.1 %copy-start.7 = (s32[12]{0:T(128)S(1)}, s32[12]{0:T(128)}, u32[]{:S(2)}) copy-start(s32[12]{0:T(128)} %param.17) | copy-start | bytes 148
  92.0 8.2 %copy-start.6 = (f32[200]{0:T(256)S(1)}, f32[200]{0:T(256)}, u32[]{:S(2)}) copy-start(f32[200]{0:T(256)} %param.20) | copy-start | bytes 2404
  92.0 8.3 %copy-start.3 = (f32[2400]{0:T(1024)S(1)}, f32[2400]{0:T(1024)}, u32[]{:S(2)}) copy-start(f32[2400]{0:T(1024)} %param.21) | copy-start | bytes 28804
  92.0 8.7 %copy-start.8 = (s32[12]{0:T(128)S(1)}, s32[12]{0:T(128)}, u32[]{:S(2)}) copy-start(s32[12]{0:T(128)} %param.18) | copy-start | bytes 148
Sparse Core Ops, SparseCore 0:
  100.2 113.3 all-reduce.4
